TPU v7x, 128 devices: a whole 4x4x4 slice. The times are simulated.
128 devices in a mesh: section: 2 (over x_hi), dp: 8 (over z, core), mp: 8 (over x_lo, y).
Axes of the slice: x: 4 (x_hi: 2, x_lo: 2; x = x_hi * 2 + x_lo), y: 4, z: 4, core: 2. Of those that a mesh axis runs over, the one named last changes fastest.
Arguments:
- inputs: bfloat16 [2, 16, 128, 4096], P('section', 'dp'), may hold values from -6 to 6
- norm_gains: bfloat16 [2, 4096], P('section'), may hold values from 0.5 to 1.5
- weights: bfloat16 [2, 4096, 4, 4096], P('section', 'dp', None, 'mp'), may hold values from -0.09375 to 0.09375
- cotangent: bfloat16 [16, 128, 4096], P('dp'), may hold values from -6 to 6
- lengths: int32 [2, 16], P(None, 'dp'), may hold values from 32 to 128, as said below
- dp_noise: float32 [2, 4096, 4, 4096], P('section', 'dp', None, 'mp'), may hold values from -6 to 6
Outputs:
- noisy_grad: float32 [2, 4096, 4, 4096], P('section', 'dp', None, 'mp')
- clip_scale: float32 [16], P('dp')
Inputs may be any that keep to these rules, and one draw needn't show every extreme that they name: `lengths`: the first example of each row has length 128.
All inputs are finite; a program needn't handle non-finite values.
Results may differ from a plain program's by a relative error of at most 0.024.
Values may be sent and summed in bfloat16 or wider, within the bound.
A program may use at most 256 MiB of HBM per device.

v0:
```python
import jax
import jax.numpy as jnp
from jax import lax
from jax.sharding import PartitionSpec as P

D = 4096
HEADS = 64
HEAD = 64


def from_partner(x, axis, distance):
    return lax.ppermute(x, axis, [(i, i ^ 1 << distance) for i in range(lax.axis_size(axis))])


def rms_norm(values_in, gain_row):
    value32 = values_in.astype(jnp.float32)
    inverse = lax.rsqrt(jnp.mean(value32 * value32, axis=-1, keepdims=True) + 1e-06)
    return (value32 * inverse * gain_row.astype(jnp.float32)).astype(jnp.bfloat16)


def project(left, right):
    return jnp.dot(left, right, preferred_element_type=jnp.float32).astype(jnp.bfloat16)


def attend(queries, key_proj, value_proj, key_mask):
    seq_len = queries.shape[0]
    query_heads = queries.reshape(seq_len, -1, HEAD)
    key_heads = key_proj.reshape(seq_len, -1, HEAD)
    value_heads = value_proj.reshape(seq_len, -1, HEAD)
    scores = jnp.einsum(
        "shd,thd->hst", query_heads, key_heads, preferred_element_type=jnp.float32
    ) * HEAD ** (-0.5)
    scores = jnp.where(key_mask[None, None, :], scores, -jnp.inf)
    attn_probs = jax.nn.softmax(scores, axis=-1)
    probs_low = attn_probs.astype(jnp.bfloat16)
    context = jnp.einsum("hst,thd->shd", probs_low, value_heads, preferred_element_type=jnp.float32)
    return (attn_probs, context.reshape(seq_len, -1).astype(jnp.bfloat16))


def attend_back(queries, key_proj, value_proj, attn_probs, grad_ctx):
    seq_len = queries.shape[0]
    query_heads = queries.reshape(seq_len, -1, HEAD)
    key_heads = key_proj.reshape(seq_len, -1, HEAD)
    value_heads = value_proj.reshape(seq_len, -1, HEAD)
    grad_heads = grad_ctx.reshape(seq_len, -1, HEAD)
    grad_probs = jnp.einsum(
        "shd,thd->hst", grad_heads, value_heads, preferred_element_type=jnp.float32
    )
    inner_sum = jnp.sum(grad_probs * attn_probs, axis=-1, keepdims=True)
    grad_scores = (attn_probs * (grad_probs - inner_sum) * HEAD ** (-0.5)).astype(jnp.bfloat16)
    probs_low = attn_probs.astype(jnp.bfloat16)
    grad_query = jnp.einsum(
        "hst,thd->shd", grad_scores, key_heads, preferred_element_type=jnp.float32
    )
    grad_key = jnp.einsum(
        "hst,shd->thd", grad_scores, query_heads, preferred_element_type=jnp.float32
    )
    grad_value = jnp.einsum(
        "hst,shd->thd", probs_low, grad_heads, preferred_element_type=jnp.float32
    )
    return (
        grad_query.reshape(seq_len, -1).astype(jnp.bfloat16),
        grad_key.reshape(seq_len, -1).astype(jnp.bfloat16),
        grad_value.reshape(seq_len, -1).astype(jnp.bfloat16),
    )


def gram(matrix):
    return jnp.dot(matrix, matrix.T, preferred_element_type=jnp.float32)


def ghost(normed, kv_rows, grad_query, grad_key, grad_value, grad_out, context):
    first = jnp.sum(gram(normed) * gram(grad_query))
    second = jnp.sum(gram(kv_rows) * (gram(grad_key) + gram(grad_value)))
    third = jnp.sum(gram(grad_out) * gram(context))
    return first + second + third


def get_row(buffer, index):
    return lax.dynamic_index_in_dim(buffer, index, 0, keepdims=False)


def put_row(buffer, value, index, valid):
    current = get_row(buffer, index)
    return lax.dynamic_update_index_in_dim(buffer, jnp.where(valid, value, current), index, 0)


def per_device(inputs, norm_gains, weights, cotangent, lengths, dp_noise):
    section_index = lax.axis_index("section")
    is_dec = section_index == 1
    micro_count = inputs.shape[1]
    seq_len = inputs.shape[2]
    width = inputs.shape[3]
    gathered = lax.all_gather(weights, "dp", axis=1, tiled=True)[0]
    inner_dev = gathered.shape[2]
    own_inputs = inputs[0]
    gain_row = norm_gains[0]
    positions = jnp.arange(seq_len)
    wide_zero = jnp.zeros((micro_count, seq_len, width), jnp.bfloat16)
    thin_zero = jnp.zeros((micro_count, seq_len, inner_dev), jnp.bfloat16)
    normed_buf, kv_buf, gout_buf = (wide_zero, wide_zero, wide_zero)
    query_buf, key_buf, value_buf, context_buf = (thin_zero, thin_zero, thin_zero, thin_zero)
    gq_buf, gk_buf, gv_buf = (thin_zero, thin_zero, thin_zero)
    probs_buf = jnp.zeros((micro_count, inner_dev // HEAD, seq_len, seq_len), jnp.float32)
    norm_parts = jnp.zeros((micro_count,), jnp.float32)
    incoming = jnp.zeros((seq_len, width), jnp.bfloat16)
    for step_num in range(micro_count + 2):
        fwd_mb = step_num - section_index
        fwd_ok = (fwd_mb >= 0) & (fwd_mb < micro_count)
        fwd_idx = jnp.clip(fwd_mb, 0, micro_count - 1)
        rows_now = get_row(own_inputs, fwd_idx)
        normed = rms_norm(rows_now, gain_row)
        kv_rows = jnp.where(is_dec, incoming, normed)
        queries = project(normed, gathered[:, 0])
        key_proj = project(kv_rows, gathered[:, 1])
        value_proj = project(kv_rows, gathered[:, 2])
        key_mask = positions < get_row(lengths[0], fwd_idx)
        attn_probs, context_new = attend(queries, key_proj, value_proj, key_mask)
        normed_buf = put_row(normed_buf, normed, fwd_idx, fwd_ok)
        kv_buf = put_row(kv_buf, kv_rows, fwd_idx, fwd_ok)
        query_buf = put_row(query_buf, queries, fwd_idx, fwd_ok)
        key_buf = put_row(key_buf, key_proj, fwd_idx, fwd_ok)
        value_buf = put_row(value_buf, value_proj, fwd_idx, fwd_ok)
        probs_buf = put_row(probs_buf, attn_probs, fwd_idx, fwd_ok)
        context_buf = put_row(context_buf, context_new, fwd_idx, fwd_ok)
        bwd_mb = step_num - 2 + section_index
        bwd_ok = (bwd_mb >= 0) & (bwd_mb < micro_count)
        bwd_idx = jnp.clip(bwd_mb, 0, micro_count - 1)
        dec_mask = (positions < get_row(lengths[1], bwd_idx)).astype(jnp.bfloat16)
        cot_rows = get_row(cotangent, bwd_idx) * dec_mask[:, None]
        grad_out = jnp.where(is_dec, cot_rows, incoming)
        grad_ctx = project(grad_out, gathered[:, 3])
        back_query = get_row(query_buf, bwd_idx)
        back_key = get_row(key_buf, bwd_idx)
        back_value = get_row(value_buf, bwd_idx)
        back_context = get_row(context_buf, bwd_idx)
        grad_query, grad_key, grad_value = attend_back(
            back_query, back_key, back_value, get_row(probs_buf, bwd_idx), grad_ctx
        )
        sq_part = ghost(
            get_row(normed_buf, bwd_idx),
            get_row(kv_buf, bwd_idx),
            grad_query,
            grad_key,
            grad_value,
            grad_out,
            back_context,
        )
        gout_buf = put_row(gout_buf, grad_out, bwd_idx, bwd_ok)
        gq_buf = put_row(gq_buf, grad_query, bwd_idx, bwd_ok)
        gk_buf = put_row(gk_buf, grad_key, bwd_idx, bwd_ok)
        gv_buf = put_row(gv_buf, grad_value, bwd_idx, bwd_ok)
        slot_hit = bwd_ok & (jnp.arange(micro_count) == bwd_idx)
        norm_parts = jnp.where(slot_hit, sq_part, norm_parts)
        if step_num < micro_count + 1:
            relay_term = lax.cond(
                is_dec,
                lambda: jnp.einsum(
                    "sj,dj->sd", grad_key, gathered[:, 1], preferred_element_type=jnp.float32
                )
                + jnp.einsum(
                    "sj,dj->sd", grad_value, gathered[:, 2], preferred_element_type=jnp.float32
                ),
                lambda: jnp.einsum(
                    "sj,dj->sd", context_new, gathered[:, 3], preferred_element_type=jnp.float32
                ),
            )
            residual = jnp.where(is_dec, 0.0, rows_now.astype(jnp.float32))
            summed_rows = lax.psum(relay_term.astype(jnp.bfloat16), "mp").astype(jnp.float32)
            payload = (summed_rows + residual).astype(jnp.bfloat16)
            incoming = from_partner(payload, "section", 0)
    sq_norm = lax.psum(norm_parts, ("section", "mp"))
    bound = jnp.sqrt(jnp.float32(8.0 * D * HEADS * HEAD))
    clip_scale = bound / (jnp.sqrt(sq_norm) + 0.01 * bound)
    totals = jnp.zeros((weights.shape[1] * lax.axis_size("dp"), 4, inner_dev), jnp.float32)
    for micro_num in range(micro_count):
        normed_cols = normed_buf[micro_num]
        kv_cols = kv_buf[micro_num]
        gout_cols = gout_buf[micro_num]
        stacked = jnp.stack(
            [
                jnp.einsum(
                    "sd,sj->dj", normed_cols, gq_buf[micro_num], preferred_element_type=jnp.float32
                ),
                jnp.einsum(
                    "sd,sj->dj", kv_cols, gk_buf[micro_num], preferred_element_type=jnp.float32
                ),
                jnp.einsum(
                    "sd,sj->dj", kv_cols, gv_buf[micro_num], preferred_element_type=jnp.float32
                ),
                jnp.einsum(
                    "sd,sj->dj",
                    gout_cols,
                    context_buf[micro_num],
                    preferred_element_type=jnp.float32,
                ),
            ],
            axis=1,
        )
        totals = totals + clip_scale[micro_num] * stacked
    summed = lax.psum_scatter(
        totals.astype(jnp.bfloat16), "dp", scatter_dimension=0, tiled=True
    ).astype(jnp.float32)
    examples_total = micro_count * lax.axis_size("dp")
    noisy_grad = (summed + dp_noise[0]) / examples_total
    return (noisy_grad[None], clip_scale)


def solution(mesh):
    placed = (
        P("section", "dp", None, None),
        P("section", None),
        P("section", "dp", None, "mp"),
        P("dp", None, None),
        P(None, "dp"),
        P("section", "dp", None, "mp"),
    )
    return jax.shard_map(
        per_device,
        mesh=mesh,
        in_specs=placed,
        out_specs=(P("section", "dp", None, "mp"), P("dp")),
        check_vma=False,
    )
```

profile of v0, /device:TPU:1, one launch (start us, length us, event | category | flops | bytes accessed | tf_op | source)
XLA Modules:
  0.0 845.7 jit_solution(15828079697014097432)
XLA Ops:
  7.2 3.3 copy.83
  24.2 2.9 fusion.165
  31.3 2.3 constant_dynamic-slice_fusion.9
  36.5 2.3 constant_dynamic-slice_fusion.1
  38.8 60.7 %all-gather.2.cloned.1.call-done = bf16[1,4096,4,512]{3,1,2,0:T(8,128)(2,1)} async-done(((bf16[1,512,4,512]{3,1,2,0:T(8,128)(2,1)}), bf16[1,4096,4,512]{3,1,2,0:T(8,128)(2,1)}) %all-gather.2.cloned.1.call-update) | async-done | bytes 16777232 | tf_op jit(solution)/shard_map/all_gather | solution.py:94
  99.5 3.3 fusion.125
  103.5 3.6 bitcast_dynamic-update-slice_fusion.20
  107.2 3.0 bitcast_dynamic-update-slice_fusion.21
  112.5 3.0 bitcast_dynamic-update-slice_fusion.19
  130.8 4.8 conditional.3
  130.8 4.8 fusion
  145.6 2.7 fusion.232
  148.2 63.0 %all-reduce.4.cloned.1.call-done = bf16[128,4096]{1,0:T(8,128)(2,1)} async-done(((bf16[128,4096]{1,0:T(8,128)(2,1)}), bf16[128,4096]{1,0:T(8,128)(2,1)}) %all-reduce.4.cloned.1.call-update) | async-done | bytes 1048592 | tf_op jit(solution)/shard_map/psum | solution.py:169
  211.2 3.8 fusion.60
  215.5 3.6 bitcast_dynamic-update-slice_fusion.17
  221.2 3.0 fusion.132
  224.9 2.4 collective-permute-start
  227.3 3.6 fusion.131
  242.6 2.8 collective-permute-done
  245.4 6.0 bitcast_dynamic-update-slice_fusion.5
  252.5 3.7 fusion.138
  259.8 2.6 fusion.380
  262.4 3.8 bitcast_dynamic-update-slice_fusion.16
  267.0 3.2 fusion.126
  291.9 2.2 convolution_bitcast_fusion.12
  299.0 4.9 conditional.4
  299.0 4.8 fusion.8
  307.5 2.6 fusion.227
  315.2 70.6 %all-reduce.6.cloned.1.call-done = bf16[128,4096]{1,0:T(8,128)(2,1)} async-done(((bf16[128,4096]{1,0:T(8,128)(2,1)}), bf16[128,4096]{1,0:T(8,128)(2,1)}) %all-reduce.6.cloned.1.call-update) | async-done | bytes 1048592 | tf_op jit(solution)/shard_map/psum | solution.py:169
  387.3 2.5 collective-permute-start.1
  389.8 2.6 fusion.168
  395.2 12.4 %collective-permute-done.1 = bf16[128,4096]{1,0:T(8,128)(2,1)S(1)} collective-permute-done((bf16[128,4096]{1,0:T(8,128)(2,1)S(1)}, bf16[128,4096]{1,0:T(8,128)(2,1)S(1)}, u32[]{:S(2)}, u32[]{:S(2)}) %collective-permute-start.1) | collective-permute-done | bytes 1048608 | tf_op jit(solution)/shard_map/ppermute | solution.py:12
  407.6 4.8 bitcast_dynamic-update-slice_fusion.4
  413.4 3.7 fusion.139
  420.7 2.7 fusion.381
  423.4 3.9 bitcast_dynamic-update-slice_fusion.13
  438.9 3.2 fusion.127
  449.7 2.2 convolution_bitcast_fusion.9
  460.9 4.8 conditional.5
  460.9 4.8 fusion.16
  466.3 2.7 fusion.222
  469.1 2.6 fusion.225
  476.4 72.0 %all-reduce.8.cloned.1.call-done = bf16[128,4096]{1,0:T(8,128)(2,1)} async-done(((bf16[128,4096]{1,0:T(8,128)(2,1)}), bf16[128,4096]{1,0:T(8,128)(2,1)}) %all-reduce.8.cloned.1.call-update) | async-done | bytes 1048592 | tf_op jit(solution)/shard_map/psum | solution.py:169
  550.0 2.9 collective-permute-start.2
  552.8 2.6 fusion.171
  558.3 12.4 %collective-permute-done.2 = bf16[128,4096]{1,0:T(8,128)(2,1)S(1)} collective-permute-done((bf16[128,4096]{1,0:T(8,128)(2,1)S(1)}, bf16[128,4096]{1,0:T(8,128)(2,1)S(1)}, u32[]{:S(2)}, u32[]{:S(2)}) %collective-permute-start.2) | collective-permute-done | bytes 1048608 | tf_op jit(solution)/shard_map/ppermute | solution.py:12
  570.7 4.8 bitcast_dynamic-update-slice_fusion.3
  576.5 3.0 fusion.140
  581.9 4.0 bitcast_dynamic-update-slice_fusion.11
  585.9 3.6 fusion.128
  604.4 5.7 convolution_bitcast_fusion.1
  610.1 5.7 convolution_bitcast_fusion.5
  615.8 5.7 convolution_bitcast_fusion.2
  621.5 5.7 convolution_bitcast_fusion.6
  629.2 5.9 convolution_bitcast_fusion
  635.1 5.7 convolution_bitcast_fusion.4
  648.2 2.6 fusion.217
  654.0 5.7 convolution_bitcast_fusion.3
  662.1 5.8 convolution_bitcast_fusion.7
  667.9 31.8 %psum.31 = f32[2]{0:T(128)S(1)} all-reduce(f32[2]{0:T(128)S(1)} %and_select_fusion.3), channel_id=1, replica_groups=mesh['section'=2,'dp'=8,'mp'=8] {'section','mp'}, use_global_device_ids=true, to_apply=%region_37.38 | all-reduce | flops 2 | bytes 16 | tf_op jit(solution)/shard_map/psum | solution.py:172
  700.3 28.8 %fusion.33 = bf16[4096,4,512]{2,0,1:T(8,128)(2,1)} fusion(f32[4096,1,512]{2,0,1:T(8,128)} %convolution_bitcast_fusion.4, f32[4096,1,512]{2,0,1:T(8,128)} %convolution_bitcast_fusion.5, f32[4096,1,512]{2,0,1:T(8,128)} %convolution_bitcast_fusion.6, f32[4096,1,512]{2,0,1:T(8,128)} %convolution_bitcast_fusion.7, f32[4096,1,512]{2,0,1:T(8,128)} %convolution_bitcast_fusion, ...), kind=kLoop, calls=%fused_computation.37 | loop fusion | flops 83886080 | bytes 83886088 | tf_op jit(solution)/shard_map/convert_element_type | solution.py:202
  729.1 100.7 %reduce-scatter.2.cloned.1.call-done = bf16[512,4,512]{2,0,1:T(8,128)(2,1)} async-done(((bf16[4096,4,512]{2,0,1:T(8,128)(2,1)}), bf16[512,4,512]{2,0,1:T(8,128)(2,1)}) %reduce-scatter.2.cloned.1.call-update) | async-done | bytes 2097168 | tf_op jit(solution)/shard_map/reduce_scatter | solution.py:201
  829.9 4.4 fusion.35
  834.3 4.7 copy.145
  (274 shorter events, 177.5 us)
Async XLA Ops:
  7.2 92.3 %all-gather.2.cloned.1.call-start = ((), (), s32[]{:S(2)}) async-start(), calls=%async_computation.1 | async-start | bytes 18874368 | tf_op jit(solution)/shard_map/all_gather | solution.py:94
  10.6 0.7 copy-start.37
  10.6 0.8 copy-start.44
  10.6 2.1 copy-start
  10.6 200.7 %all-reduce.4.cloned.1.call-start = ((), (), s32[]{:S(2)}) async-start(), calls=%async_computation.2 | async-start | bytes 2097152 | tf_op jit(solution)/shard_map/psum | solution.py:169
  21.3 86.0 %copy-start.38 = (f32[128]{0:T(128)}, f32[128]{0:T(128)S(1)}, u32[]{:S(2)}) copy-start(f32[128]{0:T(128)S(1)} %add_rsqrt_fusion.3) | copy-start | bytes 1540
  22.9 4.3 copy-start.3
  110.2 6.1 copy-start.8
  110.3 2.2 copy-start.39
  115.5 5.8 copy-start.6
  129.1 1.7 copy-start.10
  135.6 250.2 %all-reduce.6.cloned.1.call-start = ((), (), s32[]{:S(2)}) async-start(), calls=%async_computation.3 | async-start | bytes 2097152 | tf_op jit(solution)/shard_map/psum | solution.py:169
  211.2 4.3 copy-start.36
  215.5 3.6 copy-start.43
  224.9 20.6 %collective-permute-start = (bf16[128,4096]{1,0:T(8,128)(2,1)}, bf16[128,4096]{1,0:T(8,128)(2,1)}, u32[]{:S(2)}, u32[]{:S(2)}) collective-permute-start(bf16[128,4096]{1,0:T(8,128)(2,1)} %get-tuple-element.111), channel_id=1, source_target_pairs={{0,64},{64,0},{1,65},{65,1},{2,66},{66,2},{3,67},{67,3},{4,68},{68... | collective-permute-start | bytes 3145736 | tf_op jit(solution)/shard_map/ppermute | solution.py:12
  251.5 1.0 copy-start.15
  252.5 5.3 copy-start.28
  273.4 3.9 copy-start.32
  282.3 3.4 copy-start.12
  282.3 3.4 copy-start.29
  282.3 4.5 copy-start.33
  282.3 4.5 copy-start.48
  303.9 244.5 %all-reduce.8.cloned.1.call-start = ((), (), s32[]{:S(2)}) async-start(), calls=%async_computation.4 | async-start | bytes 2097152 | tf_op jit(solution)/shard_map/psum | solution.py:169
  304.0 6.2 copy-start.1
  304.7 7.4 copy-start.22
  306.3 7.3 copy-start.21
  387.3 20.3 %collective-permute-start.1 = (bf16[128,4096]{1,0:T(8,128)(2,1)S(1)}, bf16[128,4096]{1,0:T(8,128)(2,1)S(1)}, u32[]{:S(2)}, u32[]{:S(2)}) collective-permute-start(bf16[128,4096]{1,0:T(8,128)(2,1)S(1)} %fusion.67), channel_id=1, source_target_pairs={{0,64},{64,0},{1,65},{65,1},{2,66},{66,2},{3,67},{67,3},{4,68},{68... | collective-permute-start | bytes 3145736 | tf_op jit(solution)/shard_map/ppermute | solution.py:12
  392.4 15.2 %copy-start.4 = (bf16[2,128,4096]{2,1,0:T(8,128)(2,1)S(1)}, bf16[2,128,4096]{2,1,0:T(8,128)(2,1)}, u32[]{:S(2)}) copy-start(bf16[2,128,4096]{2,1,0:T(8,128)(2,1)} %param.15) | copy-start | bytes 6291460
  392.4 15.2 %copy-start.42 = (f32[128]{0:T(128)S(1)}, f32[128]{0:T(128)}, u32[]{:S(2)}) copy-start(f32[128]{0:T(128)} %add_rsqrt_fusion.1) | copy-start | bytes 1540
  392.4 15.2 %copy-start.46 = (bf16[128]{0:T(256)(128)(2,1)S(1)}, bf16[128]{0:T(256)(128)(2,1)}, u32[]{:S(2)}) copy-start(bf16[128]{0:T(256)(128)(2,1)} %compare_convert_fusion.1) | copy-start | bytes 772
  412.4 1.0 copy-start.16
  413.4 5.3 copy-start.26
  423.4 5.6 copy-start.27
  445.3 2.2 copy-start.13
  445.3 2.5 copy-start.31
  465.7 6.0 copy-start.18
  465.7 364.2 %reduce-scatter.2.cloned.1.call-start = ((), (), s32[]{:S(2)}) async-start(), calls=%async_computation.5 | async-start | bytes 18874368 | tf_op jit(solution)/shard_map/reduce_scatter | solution.py:201
  466.3 7.0 copy-start.24
  466.3 8.5 %copy-start.23 = (bf16[1,128,512]{2,1,0:T(8,128)(2,1)S(1)}, bf16[1,128,512]{2,1,0:T(8,128)(2,1)}, u32[]{:S(2)}) copy-start(bf16[1,128,512]{2,1,0:T(8,128)(2,1)} %copy.138) | copy-start | bytes 393220
  550.0 20.7 %collective-permute-start.2 = (bf16[128,4096]{1,0:T(8,128)(2,1)S(1)}, bf16[128,4096]{1,0:T(8,128)(2,1)S(1)}, u32[]{:S(2)}, u32[]{:S(2)}) collective-permute-start(bf16[128,4096]{1,0:T(8,128)(2,1)S(1)} %fusion.77), channel_id=1, source_target_pairs={{0,64},{64,0},{1,65},{65,1},{2,66},{66,2},{3,67},{67,3},{4,68},{68... | collective-permute-start | bytes 3145736 | tf_op jit(solution)/shard_map/ppermute | solution.py:12
  555.5 15.2 %copy-start.5 = (bf16[2,128,4096]{2,1,0:T(8,128)(2,1)S(1)}, bf16[2,128,4096]{2,1,0:T(8,128)(2,1)}, u32[]{:S(2)}) copy-start(bf16[2,128,4096]{2,1,0:T(8,128)(2,1)} %param.15) | copy-start | bytes 6291460
  555.5 15.2 %copy-start.41 = (f32[128]{0:T(128)S(1)}, f32[128]{0:T(128)}, u32[]{:S(2)}) copy-start(f32[128]{0:T(128)} %add_rsqrt_fusion) | copy-start | bytes 1540
  555.5 15.2 %copy-start.45 = (bf16[128]{0:T(256)(128)(2,1)S(1)}, bf16[128]{0:T(256)(128)(2,1)}, u32[]{:S(2)}) copy-start(bf16[128]{0:T(256)(128)(2,1)} %compare_convert_fusion) | copy-start | bytes 772
  575.5 1.0 copy-start.14
  576.5 3.2 copy-start.25
  576.5 3.2 copy-start.47
  579.5 6.4 copy-start.30
  579.5 2.4 copy-start.7
  579.5 2.4 copy-start.35
  581.9 4.0 copy-start.2
  585.9 7.0 copy-start.9
  589.5 9.8 %copy-start.11 = (f32[1,8,128,128]{2,3,1,0:T(8,128)S(1)}, f32[1,8,128,128]{2,3,1,0:T(8,128)}, u32[]{:S(2)}) copy-start(f32[1,8,128,128]{2,3,1,0:T(8,128)} %constant_dynamic-slice_fusion.13) | copy-start | bytes 1572868
  595.5 5.5 copy-start.19
  595.5 5.5 copy-start.17
  621.5 5.7 copy-start.34
  635.1 9.2 %copy-start.20 = (bf16[8,64,128]{2,1,0:T(8,128)(2,1)S(1)}, bf16[8,64,128]{2,1,0:T(8,128)(2,1)}, u32[]{:S(2)}) copy-start(bf16[8,64,128]{2,1,0:T(8,128)(2,1)} %copy-done.19) | copy-start | bytes 393220
  699.7 29.4 %copy-start.40 = (f32[2]{0:T(128)}, f32[2]{0:T(128)S(1)}, u32[]{:S(2)}) copy-start(f32[2]{0:T(128)S(1)} %add_divide_fusion) | copy-start | bytes 28
Sparse Core Ops, SparseCore 0:
  10.7 88.7 all-gather.1
  135.7 75.4 all-reduce.3
  304.0 81.6 all-reduce.5
  465.8 82.5 all-reduce.7
  729.2 100.5 reduce-scatter.1
where the time goes:
time: 857 us; the launch traced here: 846 us
  waiting for transfers between devices  395 us (46%)
  matrix products  202 us (24%)
  other arithmetic  95.5 us (11%)
  local copies, waits for them, and re-layouts  91.1 us (11%)
  blocking collectives  31.8 us (4%)
  between operations  22.1 us (3%)
    psum x3, waiting for transfers between devices, per_device(): lax.psum(relay_term.astype(jnp.bfloat16), 'mp').astype(jnp.float32)  206 us
    reduce_scatter x1, waiting for transfers between devices, per_device(): lax.psum_scatter(totals.astype(jnp.bfloat16), 'dp', scatter_dimension=0,...  101 us
    all_gather x1, waiting for transfers between devices, per_device(): gathered = lax.all_gather(weights, 'dp', axis=1, tiled=True)[0]  60.7 us
    dot_general x16, matrix products, project(): jnp.dot(left, right, preferred_element_type=jnp.float32)  55 us
    dynamic_update_slice x25, other arithmetic, put_row(): lax.dynamic_update_index_in_dim(buffer, jnp.where(valid, value, current),...  45.1 us
    dot_general x28, matrix products, gram(): return jnp.dot(matrix, matrix.T, preferred_element_type=jnp.float32)  42.7 us
    dynamic_slice x35, local copies, waits for them, and re-layouts, get_row(): return lax.dynamic_index_in_dim(buffer, index, 0, keepdims=False)  37.2 us
    psum x1, blocking collectives, per_device(): sq_norm = lax.psum(norm_parts, ('section', 'mp'))  31.8 us
  transfers between devices with their start and end apart: 8, of which 8 were waited for; matrix products, arithmetic and copies ran while one was open for 10% of the time, Pallas kernels for 0%

commit v1 on v0

--- a/solution.py
+++ b/solution.py
@@ -166,7 +166,9 @@
                 ),
             )
             residual = jnp.where(is_dec, 0.0, rows_now.astype(jnp.float32))
-            summed_rows = lax.psum(relay_term.astype(jnp.bfloat16), "mp").astype(jnp.float32)
+            summed_rows = jnp.sum(
+                lax.all_gather(relay_term.astype(jnp.bfloat16), "mp"), axis=0
+            ).astype(jnp.float32)
             payload = (summed_rows + residual).astype(jnp.bfloat16)
             incoming = from_partner(payload, "section", 0)
     sq_norm = lax.psum(norm_parts, ("section", "mp"))

time: 857 us -> 899 us (1.049)
  waiting for transfers between devices: 395 us -> 414 us
  other arithmetic: 95.5 us -> 113 us
  local copies, waits for them, and re-layouts: 91.1 us -> 101 us
    psum x3 -> x0, waiting for transfers between devices: 206 us -> none  [per_device(): lax.psum(relay_term.astype(jnp.bfloat16), 'mp').astype(jnp.float32)]
    all_gather x0 -> x3, waiting for transfers between devices: none -> 186 us  [per_device(): lax.all_gather(relay_term.astype(jnp.bfloat16), 'mp')]
    all_gather x1, waiting for transfers between devices: 60.7 us -> 85.2 us  [per_device(): gathered = lax.all_gather(weights, 'dp', axis=1, tiled=True)[0]]
    ppermute x3, waiting for transfers between devices: 27.6 us -> 46.2 us  [from_partner(): lax.ppermute(x, axis, [(i, i ^ 1 << distance) for i in range(lax.axis_siz...]
    reduce_sum x0 -> x3, other arithmetic: none -> 18.4 us  [per_device(): jnp.sum(lax.all_gather(relay_term.astype(jnp.bfloat16), 'mp'), axis=0)]
  transfers between devices with their start and end apart: 8 -> 8, of which waited for: 8 -> 8; matrix products, arithmetic and copies ran while one was open for 10% -> 14% of each run, Pallas kernels for 0% -> 0%
where the time goes in v1:
time: 899 us; the launch traced here: 889 us
  waiting for transfers between devices  414 us (46%)
  matrix products  200 us (22%)
  other arithmetic  113 us (13%)
  local copies, waits for them, and re-layouts  101 us (11%)
  blocking collectives  30.3 us (3%)
  between operations  22.4 us (2%)
    all_gather x3, waiting for transfers between devices, per_device(): lax.all_gather(relay_term.astype(jnp.bfloat16), 'mp')  186 us
    reduce_scatter x1, waiting for transfers between devices, per_device(): lax.psum_scatter(totals.astype(jnp.bfloat16), 'dp', scatter_dimension=0,...  96.1 us
    all_gather x1, waiting for transfers between devices, per_device(): gathered = lax.all_gather(weights, 'dp', axis=1, tiled=True)[0]  85.2 us
    dot_general x16, matrix products, project(): jnp.dot(left, right, preferred_element_type=jnp.float32)  55.6 us
    ppermute x3, waiting for transfers between devices, from_partner(): lax.ppermute(x, axis, [(i, i ^ 1 << distance) for i in range(lax.axis_siz...  46.2 us
    dynamic_update_slice x25, other arithmetic, put_row(): lax.dynamic_update_index_in_dim(buffer, jnp.where(valid, value, current),...  44.8 us
    dynamic_slice x35, local copies, waits for them, and re-layouts, get_row(): return lax.dynamic_index_in_dim(buffer, index, 0, keepdims=False)  42.2 us
    dot_general x28, matrix products, gram(): return jnp.dot(matrix, matrix.T, preferred_element_type=jnp.float32)  36.5 us
  transfers between devices with their start and end apart: 8, of which 8 were waited for; matrix products, arithmetic and copies ran while one was open for 14% of the time, Pallas kernels for 0%

profile of v1, /device:TPU:1, one launch (start us, length us, event | category | flops | bytes accessed | tf_op | source)
XLA Modules:
  0.0 889.2 jit_solution(10787314854302616078)
XLA Ops:
  7.2 3.3 copy.83
  14.2 85.2 %all-gather.8.cloned.1.call-done = bf16[1,4096,4,512]{3,1,2,0:T(8,128)(2,1)} async-done(((bf16[1,512,4,512]{3,1,2,0:T(8,128)(2,1)}), bf16[1,4096,4,512]{3,1,2,0:T(8,128)(2,1)}) %all-gather.8.cloned.1.call-update) | async-done | bytes 16777232 | tf_op jit(solution)/shard_map/all_gather | solution.py:94
  100.2 3.6 bitcast_dynamic-update-slice_fusion.20
  103.9 3.0 bitcast_dynamic-update-slice_fusion.21
  109.0 3.3 fusion.125
  112.5 3.0 bitcast_dynamic-update-slice_fusion.19
  126.4 4.8 conditional.3
  126.4 4.8 fusion
  136.8 2.6 fusion.165
  143.6 2.4 constant_dynamic-slice_fusion.9
  157.4 2.6 fusion.232
  160.0 66.7 %all-gather.10.cloned.1.call-done = bf16[1024,4096]{1,0:T(8,128)(2,1)} async-done(((bf16[128,4096]{1,0:T(8,128)(2,1)}), bf16[1024,4096]{1,0:T(8,128)(2,1)}) %all-gather.10.cloned.1.call-update) | async-done | bytes 8388624 | tf_op jit(solution)/shard_map/all_gather | solution.py:170
  226.8 6.1 reduce_sum.258
  232.9 3.7 fusion.60
  236.7 2.6 collective-permute-start
  239.3 3.6 bitcast_dynamic-update-slice_fusion.17
  245.1 3.0 fusion.131
  251.4 11.2 %collective-permute-done = bf16[128,4096]{1,0:T(8,128)(2,1)} collective-permute-done((bf16[128,4096]{1,0:T(8,128)(2,1)}, bf16[128,4096]{1,0:T(8,128)(2,1)}, u32[]{:S(2)}, u32[]{:S(2)}) %collective-permute-start) | collective-permute-done | bytes 1048608 | tf_op jit(solution)/shard_map/ppermute | solution.py:12
  262.6 6.0 bitcast_dynamic-update-slice_fusion.5
  269.6 3.6 fusion.138
  276.9 2.7 fusion.380
  279.6 3.8 bitcast_dynamic-update-slice_fusion.16
  284.2 3.9 fusion.126
  308.7 4.8 conditional.4
  308.7 4.8 fusion.8
  319.7 3.0 fusion.132
  330.5 2.7 fusion.227
  333.2 75.7 %all-gather.12.cloned.1.call-done = bf16[1024,4096]{1,0:T(8,128)(2,1)} async-done(((bf16[128,4096]{1,0:T(8,128)(2,1)}), bf16[1024,4096]{1,0:T(8,128)(2,1)}) %all-gather.12.cloned.1.call-update) | async-done | bytes 8388624 | tf_op jit(solution)/shard_map/all_gather | solution.py:170
  408.9 6.1 reduce_sum.261
  416.5 2.5 collective-permute-start.1
  419.0 2.6 fusion.168
  424.4 17.5 %collective-permute-done.1 = bf16[128,4096]{1,0:T(8,128)(2,1)S(1)} collective-permute-done((bf16[128,4096]{1,0:T(8,128)(2,1)S(1)}, bf16[128,4096]{1,0:T(8,128)(2,1)S(1)}, u32[]{:S(2)}, u32[]{:S(2)}) %collective-permute-start.1) | collective-permute-done | bytes 1048608 | tf_op jit(solution)/shard_map/ppermute | solution.py:12
  442.0 4.8 bitcast_dynamic-update-slice_fusion.4
  447.8 3.6 fusion.139
  455.1 2.7 fusion.381
  457.9 3.9 bitcast_dynamic-update-slice_fusion.13
  468.9 3.9 fusion.127
  486.5 4.9 conditional.5
  486.5 4.8 fusion.16
  516.8 2.6 fusion.230
  534.4 2.6 fusion.222
  542.9 44.0 %all-gather.14.cloned.1.call-done = bf16[1024,4096]{1,0:T(8,128)(2,1)} async-done(((bf16[128,4096]{1,0:T(8,128)(2,1)}), bf16[1024,4096]{1,0:T(8,128)(2,1)}) %all-gather.14.cloned.1.call-update) | async-done | bytes 8388624 | tf_op jit(solution)/shard_map/all_gather | solution.py:170
  586.9 6.1 reduce_sum.264
  594.5 2.7 collective-permute-start.2
  597.2 2.6 fusion.171
  602.7 17.5 %collective-permute-done.2 = bf16[128,4096]{1,0:T(8,128)(2,1)S(1)} collective-permute-done((bf16[128,4096]{1,0:T(8,128)(2,1)S(1)}, bf16[128,4096]{1,0:T(8,128)(2,1)S(1)}, u32[]{:S(2)}, u32[]{:S(2)}) %collective-permute-start.2) | collective-permute-done | bytes 1048608 | tf_op jit(solution)/shard_map/ppermute | solution.py:12
  620.2 4.8 bitcast_dynamic-update-slice_fusion.3
  626.0 3.0 fusion.140
  631.4 4.0 bitcast_dynamic-update-slice_fusion.11
  635.4 3.6 fusion.128
  653.9 5.7 convolution_bitcast_fusion.1
  659.6 5.7 convolution_bitcast_fusion.5
  665.3 5.7 convolution_bitcast_fusion.2
  671.0 5.7 convolution_bitcast_fusion.6
  678.7 5.9 convolution_bitcast_fusion
  684.7 5.7 convolution_bitcast_fusion.4
  697.6 2.6 fusion.217
  703.3 5.7 convolution_bitcast_fusion.3
  711.5 5.8 convolution_bitcast_fusion.7
  717.3 30.3 %psum.7 = f32[2]{0:T(128)S(1)} all-reduce(f32[2]{0:T(128)S(1)} %and_select_fusion.3), channel_id=1, replica_groups=mesh['section'=2,'dp'=8,'mp'=8] {'section','mp'}, use_global_device_ids=true, to_apply=%region_37.38 | all-reduce | flops 2 | bytes 16 | tf_op jit(solution)/shard_map/psum | solution.py:174
  748.2 28.8 %fusion.33 = bf16[4096,4,512]{2,0,1:T(8,128)(2,1)} fusion(f32[4096,1,512]{2,0,1:T(8,128)} %convolution_bitcast_fusion.4, f32[4096,1,512]{2,0,1:T(8,128)} %convolution_bitcast_fusion.5, f32[4096,1,512]{2,0,1:T(8,128)} %convolution_bitcast_fusion.6, f32[4096,1,512]{2,0,1:T(8,128)} %convolution_bitcast_fusion.7, f32[4096,1,512]{2,0,1:T(8,128)} %convolution_bitcast_fusion, ...), kind=kLoop, calls=%fused_computation.37 | loop fusion | flops 83886080 | bytes 83886088 | tf_op jit(solution)/shard_map/convert_element_type | solution.py:204
  777.0 96.1 %reduce-scatter.2.cloned.1.call-done = bf16[512,4,512]{2,0,1:T(8,128)(2,1)} async-done(((bf16[4096,4,512]{2,0,1:T(8,128)(2,1)}), bf16[512,4,512]{2,0,1:T(8,128)(2,1)}) %reduce-scatter.2.cloned.1.call-update) | async-done | bytes 2097168 | tf_op jit(solution)/shard_map/reduce_scatter | solution.py:203
  873.1 4.4 fusion.35
  877.5 4.7 copy.145
  (289 shorter events, 190.9 us)
Async XLA Ops:
  7.2 92.3 %all-gather.8.cloned.1.call-start = ((), (), s32[]{:S(2)}) async-start(), calls=%async_computation.1 | async-start | bytes 18874368 | tf_op jit(solution)/shard_map/all_gather | solution.py:94
  10.5 0.7 copy-start.40
  10.5 0.7 copy-start.49
  10.5 2.1 copy-start
  10.6 216.2 %all-gather.10.cloned.1.call-start = ((), (), s32[]{:S(2)}) async-start(), calls=%async_computation.3 | async-start | bytes 9437184 | tf_op jit(solution)/shard_map/all_gather | solution.py:170
  14.2 94.9 %copy-start.50 = (bf16[128]{0:T(256)(128)(2,1)}, bf16[128]{0:T(256)(128)(2,1)S(1)}, u32[]{:S(2)}) copy-start(bf16[128]{0:T(256)(128)(2,1)S(1)} %compare_convert_fusion.3) | copy-start | bytes 772
  14.2 98.3 %copy-start.41 = (f32[128]{0:T(128)}, f32[128]{0:T(128)S(1)}, u32[]{:S(2)}) copy-start(f32[128]{0:T(128)S(1)} %add_rsqrt_fusion.3) | copy-start | bytes 1540
  106.9 46.0 %copy-start.8 = (bf16[2,128,512]{2,1,0:T(8,128)(2,1)}, bf16[2,128,512]{2,1,0:T(8,128)(2,1)S(1)}, u32[]{:S(2)}) copy-start(bf16[2,128,512]{2,1,0:T(8,128)(2,1)S(1)} %get-tuple-element.148) | copy-start | bytes 786436
  112.4 8.8 copy-start.15
  115.4 5.8 copy-start.6
  121.2 1.2 copy-start.22
  122.3 0.9 copy-start.16
  131.2 277.6 %all-gather.12.cloned.1.call-start = ((), (), s32[]{:S(2)}) async-start(), calls=%async_computation.4 | async-start | bytes 9437184 | tf_op jit(solution)/shard_map/all_gather | solution.py:170
  131.5 4.0 copy-start.42
  135.5 4.0 copy-start.3
  135.5 4.0 copy-start.51
  152.9 4.3 copy-start.13
  232.9 6.3 copy-start.39
  236.7 6.2 copy-start.48
  236.7 25.9 %collective-permute-start = (bf16[128,4096]{1,0:T(8,128)(2,1)}, bf16[128,4096]{1,0:T(8,128)(2,1)}, u32[]{:S(2)}, u32[]{:S(2)}) collective-permute-start(bf16[128,4096]{1,0:T(8,128)(2,1)} %get-tuple-element.111), channel_id=1, source_target_pairs={{0,64},{64,0},{1,65},{65,1},{2,66},{66,2},{3,67},{67,3},{4,68},{68... | collective-permute-start | bytes 3145736 | tf_op jit(solution)/shard_map/ppermute | solution.py:12
  245.1 3.0 copy-start.46
  248.1 20.5 %copy-start.33 = (bf16[128,512]{1,0:T(8,128)(2,1)}, bf16[128,512]{1,0:T(8,128)(2,1)S(1)}, u32[]{:S(2)}) copy-start(bf16[128,512]{1,0:T(8,128)(2,1)S(1)} %fusion.131) | copy-start | bytes 393220
  268.6 1.0 copy-start.20
  269.6 5.3 copy-start.35
  289.1 13.0 %copy-start.17 = (bf16[128,512]{0,1:T(8,128)(2,1)}, bf16[128,512]{0,1:T(8,128)(2,1)S(1)}, u32[]{:S(2)}) copy-start(bf16[128,512]{0,1:T(8,128)(2,1)S(1)} %copy.98) | copy-start | bytes 393220
  313.5 273.4 %all-gather.14.cloned.1.call-start = ((), (), s32[]{:S(2)}) async-start(), calls=%async_computation.5 | async-start | bytes 9437184 | tf_op jit(solution)/shard_map/all_gather | solution.py:170
  319.7 3.0 copy-start.44
  322.6 0.7 copy-start.32
  416.5 25.5 %collective-permute-start.1 = (bf16[128,4096]{1,0:T(8,128)(2,1)S(1)}, bf16[128,4096]{1,0:T(8,128)(2,1)S(1)}, u32[]{:S(2)}, u32[]{:S(2)}) collective-permute-start(bf16[128,4096]{1,0:T(8,128)(2,1)S(1)} %fusion.67), channel_id=1, source_target_pairs={{0,64},{64,0},{1,65},{65,1},{2,66},{66,2},{3,67},{67,3},{4,68},{68... | collective-permute-start | bytes 3145736 | tf_op jit(solution)/shard_map/ppermute | solution.py:12
  421.6 20.3 %copy-start.4 = (bf16[2,128,4096]{2,1,0:T(8,128)(2,1)S(1)}, bf16[2,128,4096]{2,1,0:T(8,128)(2,1)}, u32[]{:S(2)}) copy-start(bf16[2,128,4096]{2,1,0:T(8,128)(2,1)} %param.15) | copy-start | bytes 6291460
  421.6 20.3 %copy-start.47 = (f32[128]{0:T(128)S(1)}, f32[128]{0:T(128)}, u32[]{:S(2)}) copy-start(f32[128]{0:T(128)} %copy-done.46) | copy-start | bytes 1540
  421.6 20.3 %copy-start.53 = (bf16[128]{0:T(256)(128)(2,1)S(1)}, bf16[128]{0:T(256)(128)(2,1)}, u32[]{:S(2)}) copy-start(bf16[128]{0:T(256)(128)(2,1)} %compare_convert_fusion.1) | copy-start | bytes 772
  446.8 1.0 copy-start.21
  477.8 3.4 copy-start.18
  491.5 381.6 %reduce-scatter.2.cloned.1.call-start = ((), (), s32[]{:S(2)}) async-start(), calls=%async_computation.2 | async-start | bytes 18874368 | tf_op jit(solution)/shard_map/reduce_scatter | solution.py:203
  514.3 5.1 copy-start.31
  514.3 6.7 copy-start.30
  514.3 8.3 copy-start.24
  514.3 8.3 copy-start.55
  514.5 13.7 %copy-start.10 = (bf16[128,8,64]{0,2,1:T(8,128)(2,1)S(1)}, bf16[128,8,64]{0,2,1:T(8,128)(2,1)}, u32[]{:S(2)}) copy-start(bf16[128,8,64]{0,2,1:T(8,128)(2,1)} %convolution_bitcast_fusion.8) | copy-start | bytes 393220
  531.1 3.0 copy-start.12
  531.1 5.9 copy-start.1
  533.9 4.2 copy-start.28
  534.2 5.5 copy-start.29
  534.4 6.9 copy-start.27
  594.5 25.7 %collective-permute-start.2 = (bf16[128,4096]{1,0:T(8,128)(2,1)S(1)}, bf16[128,4096]{1,0:T(8,128)(2,1)S(1)}, u32[]{:S(2)}, u32[]{:S(2)}) collective-permute-start(bf16[128,4096]{1,0:T(8,128)(2,1)S(1)} %fusion.77), channel_id=1, source_target_pairs={{0,64},{64,0},{1,65},{65,1},{2,66},{66,2},{3,67},{67,3},{4,68},{68... | collective-permute-start | bytes 3145736 | tf_op jit(solution)/shard_map/ppermute | solution.py:12
  599.9 20.3 %copy-start.5 = (bf16[2,128,4096]{2,1,0:T(8,128)(2,1)S(1)}, bf16[2,128,4096]{2,1,0:T(8,128)(2,1)}, u32[]{:S(2)}) copy-start(bf16[2,128,4096]{2,1,0:T(8,128)(2,1)} %param.15) | copy-start | bytes 6291460
  599.9 20.3 %copy-start.45 = (f32[128]{0:T(128)S(1)}, f32[128]{0:T(128)}, u32[]{:S(2)}) copy-start(f32[128]{0:T(128)} %copy-done.44) | copy-start | bytes 1540
  599.9 20.3 %copy-start.52 = (bf16[128]{0:T(256)(128)(2,1)S(1)}, bf16[128]{0:T(256)(128)(2,1)}, u32[]{:S(2)}) copy-start(bf16[128]{0:T(256)(128)(2,1)} %compare_convert_fusion) | copy-start | bytes 772
  625.0 1.0 copy-start.19
  626.0 3.2 copy-start.34
  626.0 3.2 copy-start.54
  629.0 6.4 copy-start.36
  629.0 2.4 copy-start.7
  629.1 2.4 copy-start.38
  631.4 4.0 copy-start.2
  635.4 7.0 copy-start.9
  639.0 9.7 %copy-start.14 = (f32[1,8,128,128]{2,3,1,0:T(8,128)S(1)}, f32[1,8,128,128]{2,3,1,0:T(8,128)}, u32[]{:S(2)}) copy-start(f32[1,8,128,128]{2,3,1,0:T(8,128)} %constant_dynamic-slice_fusion.13) | copy-start | bytes 1572868
  645.0 5.5 copy-start.25
  645.0 5.5 copy-start.23
  671.0 5.7 copy-start.37
  684.7 9.1 %copy-start.26 = (bf16[8,64,128]{2,1,0:T(8,128)(2,1)S(1)}, bf16[8,64,128]{2,1,0:T(8,128)(2,1)}, u32[]{:S(2)}) copy-start(bf16[8,64,128]{2,1,0:T(8,128)(2,1)} %copy-done.25) | copy-start | bytes 393220
  747.5 29.4 %copy-start.43 = (f32[2]{0:T(128)}, f32[2]{0:T(128)S(1)}, u32[]{:S(2)}) copy-start(f32[2]{0:T(128)S(1)} %add_divide_fusion) | copy-start | bytes 28
Sparse Core Ops, SparseCore 0:
  10.7 88.7 all-gather.7
  131.3 95.3 all-gather.9
  313.6 95.1 all-gather.11
  491.6 95.2 all-gather.13
  777.1 95.9 reduce-scatter.1
